TPU v7x, 32 devices: a whole 2x2x4 slice. The times are simulated.
32 devices in a mesh: ctx: 8 (over z, x), exp: 4 (over y, core).
Axes of the slice: x: 2, y: 2, z: 4, core: 2. Of those that a mesh axis runs over, the one named last changes fastest.
Arguments:
- residual: bfloat16 [4, 1024, 2048], P('exp', 'ctx'), may hold values from -54 to 54
- queries: bfloat16 [4, 1024, 2048], P('exp', 'ctx'), may hold values from -160 to 160
- key_states: bfloat16 [4, 1024, 256], P('exp', 'ctx'), may hold values from -6.1 to 6.1
- value_states: bfloat16 [4, 1024, 256], P('exp', 'ctx'), may hold values from -6 to 6
- expert_ids: int32 [4, 1024, 1], P('exp', 'ctx'), may hold values from 0 to 7; in each aligned block of 128 rows (0 to 127, 128 to 255, ..., all dimensions but the last counted through in order) at most 32 rows name the same one
- route_weight: float32 [4, 1024, 1], P('exp', 'ctx'), may hold values from 0.2 to 1
- gate_weight: bfloat16 [4, 8, 192, 2048], P('exp', 'ctx'), may hold values from -0.125 to 0.125
- up_weight: bfloat16 [4, 8, 192, 2048], P('exp', 'ctx'), may hold values from -0.125 to 0.125
- down_weight: bfloat16 [4, 8, 192, 2048], P('exp', 'ctx'), may hold values from -0.21875 to 0.21875
Outputs:
- output: bfloat16 [4, 1024, 2048], P('exp', 'ctx')
Inputs may be any that keep to these rules, and one draw needn't show every extreme that they name: `expert_ids`: within each aligned block of 128 rows (sequence by sequence, positions in order), which is the rows of one device, no expert is named more than 32 times, a bound that some block reaches; every expert is named somewhere.
All inputs are finite; a program needn't handle non-finite values.
Results may differ from a plain program's by a relative error of at most 0.003.
Values may be sent and summed in bfloat16 or wider, within the bound.
No kernel may reach another device: no remote copies, remote signals or barrier semaphores. Data moves between devices by JAX's collectives and lax.ppermute only.
A program may use at most 64 MiB of HBM per device.

v0:
```python
from functools import partial
import math
import jax
import jax.numpy as jnp
from jax import lax
from jax.sharding import PartitionSpec as P

HD = 128
HEADS = 16
KV_HEADS = 2
PIECES = 4
TOPK = 1
negative_fill = -1e30
epsilon = 1e-06


def contract_rows(left_rows, weight_rows):
    return lax.dot_general(
        left_rows, weight_rows, (((1,), (1,)), ((), ())), preferred_element_type=jnp.float32
    )


def to_groups(half_block, heads_kv, group_size, head_dim):
    token_count = half_block.shape[0]
    shaped = half_block.reshape(token_count, heads_kv, group_size, head_dim)
    return jnp.transpose(shaped, (1, 0, 2, 3)).reshape(heads_kv, token_count * group_size, head_dim)


def keep_current(current):
    return current


def block_update(current, query_rows, query_pos, key_block, value_block, key_start, score_scale):
    running_max, running_total, accumulated = current
    scores = (
        jnp.einsum("gqd,kgd->gqk", query_rows, key_block, preferred_element_type=jnp.float32)
        * score_scale
    )
    key_pos = key_start + jnp.arange(key_block.shape[0], dtype=jnp.int32)
    allowed = key_pos[None, None, :] <= query_pos[None, :, None]
    scores = jnp.where(allowed, scores, negative_fill)
    new_max = jnp.maximum(running_max, jnp.max(scores, axis=-1))
    rescale = jnp.exp(running_max - new_max)
    exponent = jnp.where(allowed, jnp.exp(scores - new_max[..., None]), 0.0)
    new_total = running_total * rescale + jnp.sum(exponent, axis=-1)
    product = jnp.einsum(
        "gqk,kgd->gqd",
        exponent.astype(jnp.bfloat16),
        value_block,
        preferred_element_type=jnp.float32,
    )
    return (new_max, new_total, accumulated * rescale[..., None] + product)


def make_folder(query_sets, position_sets, last_positions, heads_kv, head_dim, score_scale):

    def fold_keys(running, key_piece, first_key):
        key_part, value_part = key_piece
        key_count = key_part.shape[1]
        key_width = math.gcd(key_count, 512)
        key_rows = key_part.reshape(key_count, heads_kv, head_dim)
        value_rows = value_part.reshape(key_count, heads_kv, head_dim)

        def one_block(block_index, current_sets):
            offset = block_index * key_width
            key_block = lax.dynamic_slice_in_dim(key_rows, offset, key_width, 0)
            value_block = lax.dynamic_slice_in_dim(value_rows, offset, key_width, 0)
            updated = []
            for current, query_rows, query_pos, last_pos in zip(
                current_sets, query_sets, position_sets, last_positions
            ):
                step_fn = partial(
                    block_update,
                    query_rows=query_rows,
                    query_pos=query_pos,
                    key_block=key_block,
                    value_block=value_block,
                    key_start=offset,
                    score_scale=score_scale,
                )
                updated.append(lax.cond(offset <= last_pos, step_fn, keep_current, current))
            return tuple(updated)

        return lax.fori_loop(0, key_count // key_width, one_block, running)

    return fold_keys


def finish(current, token_count, heads_kv, group_size, head_dim):
    running_max, running_total, accumulated = current
    result = accumulated / running_total[..., None]
    shaped = result.reshape(heads_kv, token_count, group_size, head_dim)
    return (
        jnp.transpose(shaped, (1, 0, 2, 3))
        .reshape(token_count, heads_kv * group_size * head_dim)
        .astype(jnp.bfloat16)
    )


def shards(
    residual,
    queries,
    key_states,
    value_states,
    expert_ids,
    route_weight,
    gate_weight,
    up_weight,
    down_weight,
):
    ctx_count = lax.axis_size("ctx")
    exp_count = lax.axis_size("exp")
    ctx_rank = lax.axis_index("ctx")
    tok_rows = residual.shape[1]
    half_rows = tok_rows // 2
    group_size = HEADS // KV_HEADS
    score_scale = 1.0 / math.sqrt(HD)
    local_queries = queries[0]
    first_half = local_queries[:half_rows]
    second_half = local_queries[half_rows:]
    first_start = ctx_rank * tok_rows
    second_start = first_start + half_rows
    offsets = jnp.repeat(jnp.arange(half_rows, dtype=jnp.int32), group_size)
    query_sets = (
        to_groups(first_half, KV_HEADS, group_size, HD),
        to_groups(second_half, KV_HEADS, group_size, HD),
    )
    position_sets = (first_start + offsets, second_start + offsets)
    last_positions = (first_start + half_rows - 1, second_start + half_rows - 1)
    row_total = half_rows * group_size
    empty_state = (
        jnp.full((KV_HEADS, row_total), negative_fill, jnp.float32),
        jnp.zeros((KV_HEADS, row_total), jnp.float32),
        jnp.zeros((KV_HEADS, row_total, HD), jnp.float32),
    )
    folder = make_folder(query_sets, position_sets, last_positions, KV_HEADS, HD, score_scale)
    final_sets = folder(
        (empty_state, empty_state),
        (
            lax.all_gather(key_states, "ctx", axis=1, tiled=True),
            lax.all_gather(value_states, "ctx", axis=1, tiled=True),
        ),
        jnp.int32(0),
    )
    first_out = finish(final_sets[0], half_rows, KV_HEADS, group_size, HD)
    second_out = finish(final_sets[1], half_rows, KV_HEADS, group_size, HD)
    attention = jnp.concatenate([first_out, second_out], axis=0)
    summed = residual[0].astype(jnp.float32) + lax.optimization_barrier(attention).astype(
        jnp.float32
    )
    normed = (
        summed * lax.rsqrt(jnp.mean(summed * summed, axis=-1, keepdims=True) + epsilon)
    ).astype(jnp.bfloat16)
    width_model = normed.shape[1]
    experts_each = ctx_count // PIECES
    expert_total = experts_each * exp_count
    pair_count = tok_rows * TOPK
    capacity = max(2, 2 * tok_rows * TOPK // expert_total)
    flat_ids = expert_ids[0].reshape(pair_count)
    onehot = (flat_ids[:, None] == jnp.arange(expert_total, dtype=jnp.int32)[None, :]).astype(
        jnp.int32
    )
    earlier = jnp.cumsum(onehot, axis=0) - onehot
    slot_index = jnp.sum(earlier * onehot, axis=1)
    owner_index = flat_ids // experts_each
    local_expert = flat_ids % experts_each
    target = (local_expert * exp_count + owner_index) * capacity + slot_index
    pair_token = jnp.arange(pair_count, dtype=jnp.int32) // TOPK
    slot_total = expert_total * capacity
    slot_table = jnp.full((slot_total,), tok_rows, jnp.int32).at[target].set(pair_token)
    padded = jnp.concatenate([normed, jnp.zeros((1, width_model), jnp.bfloat16)], axis=0)
    outgoing = padded[slot_table].reshape(experts_each, exp_count, capacity, width_model)
    arrived = lax.all_to_all(outgoing, "exp", split_axis=1, concat_axis=1, tiled=True)
    copies = jnp.broadcast_to(
        arrived[:, None], (experts_each, PIECES, exp_count, capacity, width_model)
    ).reshape(ctx_count, exp_count * capacity, width_model)
    gate_piece = gate_weight[0, 0]
    up_piece = up_weight[0, 0]
    down_piece = down_weight[0, 0]
    received = lax.all_to_all(copies, "ctx", split_axis=0, concat_axis=0, tiled=True)
    sources = received.shape[0]
    item_count = received.shape[1]
    flat_rows = received.reshape(sources * item_count, width_model)
    gate_part = contract_rows(flat_rows, gate_piece)
    up_part = contract_rows(flat_rows, up_piece)
    active = (jax.nn.silu(gate_part) * up_part).astype(jnp.bfloat16)
    partial_out = jnp.dot(active, down_piece, preferred_element_type=jnp.float32).astype(
        jnp.bfloat16
    )
    returned = lax.all_to_all(
        partial_out.reshape(sources, item_count, width_model),
        "ctx",
        split_axis=0,
        concat_axis=0,
        tiled=True,
    )
    piece_sum = jnp.sum(
        returned.reshape(experts_each, PIECES, exp_count, capacity, width_model).astype(
            jnp.float32
        ),
        axis=1,
    ).astype(jnp.bfloat16)
    arrived_back = lax.all_to_all(piece_sum, "exp", split_axis=1, concat_axis=1, tiled=True)
    gathered = arrived_back.reshape(slot_total, width_model)[target].astype(jnp.float32)
    weighted = gathered * route_weight[0]
    mixture = jnp.sum(weighted.reshape(tok_rows, TOPK, width_model), axis=1)
    return (summed + mixture).astype(jnp.bfloat16)[None]


def solution(mesh):
    in_specs = (
        P("exp", "ctx", None),
        P("exp", "ctx", None),
        P("exp", "ctx", None),
        P("exp", "ctx", None),
        P("exp", "ctx", None),
        P("exp", "ctx", None),
        P("exp", "ctx", None, None),
        P("exp", "ctx", None, None),
        P("exp", "ctx", None, None),
    )
    out_specs = P("exp", "ctx", None)
    return jax.shard_map(shards, mesh=mesh, in_specs=in_specs, out_specs=out_specs, check_vma=False)
```

profile of v0, /device:TPU:0, one launch (start us, length us, event | category | flops | bytes accessed | tf_op | source)
XLA Modules:
  0.0 328.2 jit_solution(8292580245410848761)
XLA Ops:
  0.0 1.1 slice_bitcast_fusion
  1.3 0.1 copy.41
  1.4 29.6 %all_gather.6 = bf16[1,1024,256]{1,2,0:T(8,128)(2,1)S(1)} all-gather(bf16[1,128,256]{1,2,0:T(8,128)(2,1)S(1)} %copy.41), channel_id=1, replica_groups=mesh['ctx'=8,'exp'=4] {'ctx'}, dimensions={1}, use_global_device_ids=true | all-gather | bytes 589824 | tf_op jit(solution)/shard_map/all_gather | solution.py:140
  31.0 0.1 copy.42
  31.1 27.8 %all_gather.7 = bf16[1,1024,256]{1,2,0:T(8,128)(2,1)S(1)} all-gather(bf16[1,128,256]{1,2,0:T(8,128)(2,1)S(1)} %copy.42), channel_id=1, replica_groups=mesh['ctx'=8,'exp'=4] {'ctx'}, dimensions={1}, use_global_device_ids=true | all-gather | bytes 589824 | tf_op jit(solution)/shard_map/all_gather | solution.py:141
  58.9 0.1 copy_bitcast_fusion.2
  59.0 0.8 broadcast_in_dim.78
  59.8 0.8 broadcast_in_dim.78.clone
  60.6 9.5 %while.24 = (s32[]{:T(128)}, f32[2,512]{1,0:T(2,128)S(1)}, f32[2,512]{1,0:T(2,128)S(1)}, f32[2,512,128]{2,1,0:T(8,128)}, f32[2,512]{1,0:T(2,128)S(1)}, /*index=5...) while((s32[]{:T(128)}, f32[2,512]{1,0:T(2,128)S(1)}, ...), condition=%wide.region_9.10_spmd.clone, body=%wide.region_0.9_spmd.clone.sunk | while | flops 551557120 | bytes 29000316 | solution.py:84
  60.7 0.2 copy.69
  60.9 0.2 copy.70
  61.1 0.0 copy-start.3
  61.1 3.4 %conditional.7 = ((f32[2,512]{1,0:T(2,128)S(1)}, f32[2,512]{1,0:T(2,128)S(1)}, f32[2,512,128]{2,1,0:T(8,128)})) conditional(s32[]{:T(128)} %convert_element_type.131, (f32[2,512]{1,0:T(2,128)S(1)}, f32[2,512]{1,0:T(2,128)S(1)}, f32[2,512,128]{2,1,0:T(8,128)}) %tuple.67, (s32[]{:T(128)}, s32[]{:T(128)}, bf16[2,512,128]{2,1,0:T(8,128)(2,1)S(1)}, ...), branch_computations={%region_5.5_spmd, %region_6.8_spmd} | conditional | flops 275778560 | bytes 13449312 | solution.py:81
  61.1 0.1 add.216
  61.2 0.2 broadcast_compare_fusion.1
  61.5 0.0 copy-start.5
  61.5 0.5 fusion.15
  62.0 0.6 fusion.17
  62.6 1.1 convolution_add_fusion.1
  63.7 0.8 copy-done.6
  64.5 2.6 conditional.6
  64.6 0.1 add.213
  64.7 0.2 broadcast_compare_fusion
  64.9 0.5 fusion.4
  65.4 0.6 fusion.6
  66.0 1.1 convolution_add_fusion
  67.1 0.0 copy-start.4
  67.1 0.8 copy-done.4
  68.0 0.2 copy.69
  68.1 0.2 copy.70
  68.3 0.0 copy-start.3
  68.4 1.0 copy-done.3
  69.4 0.8 copy-done.4
  70.2 1.3 fusion.39
  71.5 0.0 copy-start.1
  71.5 0.1 copy.66
  71.6 0.2 fusion.40
  71.9 0.0 copy-start.10
  71.9 0.1 copy.65
  72.0 0.5 copy-done.1
  72.5 0.3 multiply_reduce_fusion
  72.8 0.2 multiply_convert_fusion
  73.0 0.1 fusion.41
  73.1 0.2 reduce_window_sum.11
  73.2 0.2 select_reduce_fusion
  73.5 1.0 scatter_custom_fusion
  74.5 1.4 gather_fusion
  75.9 0.1 copy.49
  76.0 17.1 %all_to_all.20 = bf16[2,4,32,2048]{3,2,0,1:T(8,128)(2,1)S(1)} all-to-all(bf16[2,4,32,2048]{3,2,0,1:T(8,128)(2,1)S(1)} %copy.49), channel_id=1, replica_groups=mesh['ctx'=8,'exp'=4] {'exp'}, dimensions={1} | all-to-all | bytes 2097152 | tf_op jit(solution)/shard_map/all_to_all | solution.py:173
  93.1 0.1 copy.50
  93.1 0.5 broadcast_in_dim.83
  93.7 99.7 %all_to_all.21 = bf16[8,128,2048]{2,1,0:T(8,128)(2,1)S(1)} all-to-all(bf16[8,128,2048]{2,1,0:T(8,128)(2,1)S(1)} %bitcast.91), channel_id=1, replica_groups=mesh['ctx'=8,'exp'=4] {'ctx'}, dimensions={0} | all-to-all | bytes 8388608 | tf_op jit(solution)/shard_map/all_to_all | solution.py:180
  193.4 2.0 copy-done.2
  195.4 2.5 fusion.30
  197.9 7.1 %convolution_convert_fusion = bf16[1024,2048]{1,0:T(8,128)(2,1)} fusion(bf16[1024,2048]{1,0:T(8,128)(2,1)} %bitcast.97, bf16[1,1,192,2048]{3,2,1,0:T(8,128)(2,1)S(1)} %copy-done, bf16[1,1,192,2048]{3,2,1,0:T(8,128)(2,1)S(1)} %copy-done.13, f32[1024,192]{0,1:T(8,128)} %fusion.30), kind=kOutput, calls=%fused_computation.43 | convolution fusion | flops 1613889536 | bytes 10747904 | tf_op jit(solution)/shard_map/dot_general | solution.py:187
  205.0 97.0 %all_to_all.22 = bf16[8,128,2048]{2,1,0:T(8,128)(2,1)} all-to-all(bf16[8,128,2048]{2,1,0:T(8,128)(2,1)} %bitcast.98), channel_id=1, replica_groups=mesh['ctx'=8,'exp'=4] {'ctx'}, dimensions={0} | all-to-all | bytes 8388608 | tf_op jit(solution)/shard_map/all_to_all | solution.py:190
  302.0 3.1 reduce_sum.57
  305.0 1.1 copy.51
  306.1 4.2 %all-to-all-start.3 = ((bf16[2,4,32,2048]{3,2,0,1:T(8,128)(2,1)}), bf16[2,4,32,2048]{3,2,0,1:T(8,128)(2,1)}, u32[]{:S(2)}, u32[]{:S(2)}) async-start(bf16[2,4,32,2048]{3,2,0,1:T(8,128)(2,1)} %copy.51), calls=%async_computation.3 | async-start | bytes 2097152 | tf_op jit(solution)/shard_map/all_to_all | solution.py:203
  310.4 14.5 %all-to-all-done.3 = bf16[2,4,32,2048]{3,2,0,1:T(8,128)(2,1)} async-done(((bf16[2,4,32,2048]{3,2,0,1:T(8,128)(2,1)}), bf16[2,4,32,2048]{3,2,0,1:T(8,128)(2,1)}, u32[]{:S(2)}, u32[]{:S(2)}) %all-to-all-start.3) | async-done | bytes 1048608 | tf_op jit(solution)/shard_map/all_to_all | solution.py:203
  324.9 1.3 copy.52
  326.2 0.0 copy-start.11
  326.2 0.9 gather_fusion.1
  327.1 1.1 fusion.37
  (53 shorter events, 0.5 us)
Async XLA Ops:
  0.0 197.9 %copy-start = (bf16[1,1,192,2048]{3,2,1,0:T(8,128)(2,1)S(1)}, bf16[1,1,192,2048]{3,2,1,0:T(8,128)(2,1)}, u32[]{:S(2)}) copy-start(bf16[1,1,192,2048]{3,2,1,0:T(8,128)(2,1)} %param.23) | copy-start | bytes 2359300
  0.0 1.3 copy-start.8
  0.0 30.9 %copy-start.9 = (bf16[1,128,256]{2,1,0:T(8,128)(2,1)S(1)}, bf16[1,128,256]{2,1,0:T(8,128)(2,1)}, u32[]{:S(2)}) copy-start(bf16[1,128,256]{2,1,0:T(8,128)(2,1)} %param.18) | copy-start | bytes 196612
  61.1 3.4 %copy-start.3 = (f32[2,512,128]{2,1,0:T(8,128)S(1)}, f32[2,512,128]{2,1,0:T(8,128)}, u32[]{:S(2)}) copy-start(f32[2,512,128]{2,1,0:T(8,128)} %get-tuple-element.613) | copy-start | bytes 1572868 | tf_op jit(solution)/shard_map/while
  61.5 1.2 copy-start.5
  63.7 0.8 copy-start.6
  67.1 0.8 copy-start.4
  68.3 1.0 copy-start.3
  69.4 0.8 copy-start.4
  70.2 1.5 copy-start.7
  71.5 1.0 copy-start.1
  71.9 1.1 copy-start.10
  93.7 101.7 %copy-start.12 = (bf16[1,1,192,2048]{3,2,1,0:T(8,128)(2,1)S(1)}, bf16[1,1,192,2048]{3,2,1,0:T(8,128)(2,1)}, u32[]{:S(2)}) copy-start(bf16[1,1,192,2048]{3,2,1,0:T(8,128)(2,1)} %param.21) | copy-start | bytes 2359300
  193.4 2.0 copy-start.2
  195.4 2.5 copy-start.13
  306.1 18.8 %all-to-all-start.3 = ((bf16[2,4,32,2048]{3,2,0,1:T(8,128)(2,1)}), bf16[2,4,32,2048]{3,2,0,1:T(8,128)(2,1)}, u32[]{:S(2)}, u32[]{:S(2)}) async-start(bf16[2,4,32,2048]{3,2,0,1:T(8,128)(2,1)} %copy.51), calls=%async_computation.3 | async-start | bytes 2097152 | tf_op jit(solution)/shard_map/all_to_all | solution.py:203
  326.2 1.0 copy-start.11
where the time goes:
time: 329 us; the launch traced here: 328 us
  blocking collectives  271 us (82%)
  local copies, waits for them, and re-layouts  16.7 us (5%)
  waiting for transfers between devices  14.5 us (4%)
  matrix products  12.8 us (4%)
  other arithmetic  8.21 us (2%)
  starting transfers between devices  4.23 us (1%)
    all_to_all x1, blocking collectives, shards(): lax.all_to_all(copies, 'ctx', split_axis=0, concat_axis=0, tiled=True)  99.7 us
    all_to_all x1, blocking collectives, shards(): lax.all_to_all(partial_out.reshape(sources, item_count, width_model), 'ct...  97 us
    all_gather x1, blocking collectives, shards(): lax.all_gather(key_states, 'ctx', axis=1, tiled=True)  29.6 us
    all_gather x1, blocking collectives, shards(): lax.all_gather(value_states, 'ctx', axis=1, tiled=True)  27.8 us
    all_to_all x1, blocking collectives, shards(): lax.all_to_all(outgoing, 'exp', split_axis=1, concat_axis=1, tiled=True)  17.1 us
    all_to_all x1, waiting for transfers between devices, shards(): lax.all_to_all(piece_sum, 'exp', split_axis=1, concat_axis=1, tiled=True)  14.5 us
    dot_general x1, matrix products, shards(): jnp.dot(active, down_piece, preferred_element_type=jnp.float32)  7.06 us
  transfers between devices with their start and end apart: 1, of which 1 were waited for; matrix products, arithmetic and copies ran while one was open for 0% of the time, Pallas kernels for 0%

commit v1 on v0

--- a/solution.py
+++ b/solution.py
@@ -12,6 +12,29 @@
 TOPK = 1
 negative_fill = -1e30
 epsilon = 1e-06
+
+
+def in_blocks(shard, dim, size):
+    before, after = (shard.shape[:dim], shard.shape[dim + 1 :])
+    return jnp.moveaxis(shard.reshape(*before, size, -1, *after), dim, 0)
+
+
+def laid_out(pieces, dim):
+    lengths = list(pieces.shape[1:])
+    lengths[dim] *= pieces.shape[0]
+    return jnp.moveaxis(pieces, 0, dim).reshape(lengths)
+
+
+def exchange_directly(x, axis, split_dim, concat_dim):
+    size, index = (lax.axis_size(axis), lax.axis_index(axis))
+    blocks = in_blocks(x, split_dim, size)
+    result = blocks
+    for step in range(1, size):
+        target, source = ((index + step) % size, (index - step) % size)
+        sent = lax.dynamic_index_in_dim(blocks, target, 0)
+        other = lax.ppermute(sent, axis, [(i, (i + step) % size) for i in range(size)])
+        result = lax.dynamic_update_slice_in_dim(result, other, source, axis=0)
+    return laid_out(result, concat_dim)
 
 
 def contract_rows(left_rows, weight_rows):
@@ -200,7 +223,7 @@
         ),
         axis=1,
     ).astype(jnp.bfloat16)
-    arrived_back = lax.all_to_all(piece_sum, "exp", split_axis=1, concat_axis=1, tiled=True)
+    arrived_back = exchange_directly(piece_sum, "exp", 1, 1)
     gathered = arrived_back.reshape(slot_total, width_model)[target].astype(jnp.float32)
     weighted = gathered * route_weight[0]
     mixture = jnp.sum(weighted.reshape(tok_rows, TOPK, width_model), axis=1)

time: 329 us -> 325 us (0.988)
  blocking collectives: 271 us -> 174 us
  waiting for transfers between devices: 14.5 us -> 101 us
    all_to_all x1 -> x0, blocking collectives: 97 us -> none  [shards(): lax.all_to_all(partial_out.reshape(sources, item_count, width_model), 'ct...]
    all_to_all x1, waiting for transfers between devices: 14.5 us -> 92.2 us  [shards(): lax.all_to_all(partial_out.reshape(sources, item_count, width_model), 'ct...]
    ppermute x0 -> x3, waiting for transfers between devices: none -> 8.52 us  [exchange_directly(): lax.ppermute(sent, axis, [(i, (i + step) % size) for i in range(size)])]
  transfers between devices with their start and end apart: 1 -> 4, of which waited for: 1 -> 3; matrix products, arithmetic and copies ran while one was open for 0% -> 1% of each run, Pallas kernels for 0% -> 0%
where the time goes in v1:
time: 325 us; the launch traced here: 322 us
  blocking collectives  174 us (54%)
  waiting for transfers between devices  101 us (31%)
  local copies, waits for them, and re-layouts  19.2 us (6%)
  matrix products  12.8 us (4%)
  other arithmetic  8.22 us (3%)
  starting transfers between devices  6.62 us (2%)
    all_to_all x1, blocking collectives, shards(): lax.all_to_all(copies, 'ctx', split_axis=0, concat_axis=0, tiled=True)  99.7 us
    all_to_all x1, waiting for transfers between devices, shards(): lax.all_to_all(partial_out.reshape(sources, item_count, width_model), 'ct...  92.2 us
    all_gather x1, blocking collectives, shards(): lax.all_gather(key_states, 'ctx', axis=1, tiled=True)  29.6 us
    all_gather x1, blocking collectives, shards(): lax.all_gather(value_states, 'ctx', axis=1, tiled=True)  27.8 us
    all_to_all x1, blocking collectives, shards(): lax.all_to_all(outgoing, 'exp', split_axis=1, concat_axis=1, tiled=True)  17.1 us
    ppermute x3, waiting for transfers between devices, exchange_directly(): lax.ppermute(sent, axis, [(i, (i + step) % size) for i in range(size)])  8.52 us
    dot_general x1, matrix products, shards(): jnp.dot(active, down_piece, preferred_element_type=jnp.float32)  7.05 us
  transfers between devices with their start and end apart: 4, of which 3 were waited for; matrix products, arithmetic and copies ran while one was open for 1% of the time, Pallas kernels for 0%

profile of v1, /device:TPU:0, one launch (start us, length us, event | category | flops | bytes accessed | tf_op | source)
XLA Modules:
  0.0 322.4 jit_solution(9100023066045422515)
XLA Ops:
  0.0 1.2 slice_bitcast_fusion
  1.3 0.1 copy.28
  1.4 29.6 %all_gather.6 = bf16[1,1024,256]{1,2,0:T(8,128)(2,1)S(1)} all-gather(bf16[1,128,256]{1,2,0:T(8,128)(2,1)S(1)} %copy.28), channel_id=1, replica_groups=mesh['ctx'=8,'exp'=4] {'ctx'}, dimensions={1}, use_global_device_ids=true | all-gather | bytes 589824 | tf_op jit(solution)/shard_map/all_gather | solution.py:163
  31.0 0.1 copy.29
  31.1 27.8 %all_gather.7 = bf16[1,1024,256]{1,2,0:T(8,128)(2,1)S(1)} all-gather(bf16[1,128,256]{1,2,0:T(8,128)(2,1)S(1)} %copy.29), channel_id=1, replica_groups=mesh['ctx'=8,'exp'=4] {'ctx'}, dimensions={1}, use_global_device_ids=true | all-gather | bytes 589824 | tf_op jit(solution)/shard_map/all_gather | solution.py:164
  58.9 0.1 copy_bitcast_fusion.2
  59.0 0.8 broadcast_in_dim.78
  59.8 0.8 broadcast_in_dim.78.clone
  60.7 9.5 %while.24 = (s32[]{:T(128)}, f32[2,512]{1,0:T(2,128)S(1)}, f32[2,512]{1,0:T(2,128)S(1)}, f32[2,512,128]{2,1,0:T(8,128)}, f32[2,512]{1,0:T(2,128)S(1)}, /*index=5...) while((s32[]{:T(128)}, f32[2,512]{1,0:T(2,128)S(1)}, ...), condition=%wide.region_9.10_spmd.clone, body=%wide.region_0.9_spmd.clone.sunk | while | flops 551557120 | bytes 29000316 | solution.py:107
  60.7 0.2 copy.54
  60.9 0.2 copy.55
  61.1 0.0 copy-start.3
  61.1 3.4 %conditional.7 = ((f32[2,512]{1,0:T(2,128)S(1)}, f32[2,512]{1,0:T(2,128)S(1)}, f32[2,512,128]{2,1,0:T(8,128)})) conditional(s32[]{:T(128)} %convert_element_type.131, (f32[2,512]{1,0:T(2,128)S(1)}, f32[2,512]{1,0:T(2,128)S(1)}, f32[2,512,128]{2,1,0:T(8,128)}) %tuple.68, (s32[]{:T(128)}, s32[]{:T(128)}, bf16[2,512,128]{2,1,0:T(8,128)(2,1)S(1)}, ...), branch_computations={%region_5.5_spmd, %region_6.8_spmd} | conditional | flops 275778560 | bytes 13449312 | solution.py:104
  61.2 0.1 add.281
  61.2 0.2 broadcast_compare_fusion.1
  61.5 0.0 copy-start.5
  61.5 0.5 fusion.15
  62.1 0.6 fusion.17
  62.6 1.1 convolution_add_fusion.1
  63.7 0.8 copy-done.6
  64.5 2.6 conditional.6
  64.6 0.1 add.278
  64.7 0.2 broadcast_compare_fusion
  64.9 0.5 fusion.4
  65.5 0.6 fusion.6
  66.0 1.1 convolution_add_fusion
  67.2 0.8 copy-done.4
  68.0 0.2 copy.54
  68.2 0.2 copy.55
  68.4 1.0 copy-done.3
  69.4 0.8 copy-done.4
  70.2 1.3 fusion.39
  71.5 0.0 copy-start.1
  71.6 0.1 copy.51
  71.7 0.2 fusion.40
  71.9 0.1 copy.50
  72.1 0.5 copy-done.1
  72.6 0.3 multiply_reduce_fusion
  72.8 0.2 multiply_convert_fusion
  73.0 0.1 fusion.41
  73.1 0.2 reduce_window_sum.11
  73.3 0.2 select_reduce_fusion
  73.5 1.0 scatter_custom_fusion
  74.5 2.3 gather_fusion
  76.9 1.3 copy.36
  78.2 17.1 %all_to_all.15 = bf16[2,4,32,2048]{3,2,0,1:T(8,128)(2,1)S(1)} all-to-all(bf16[2,4,32,2048]{3,2,0,1:T(8,128)(2,1)S(1)} %copy.36), channel_id=1, replica_groups=mesh['ctx'=8,'exp'=4] {'exp'}, dimensions={1} | all-to-all | bytes 2097152 | tf_op jit(solution)/shard_map/all_to_all | solution.py:196
  95.2 0.1 copy.37
  95.3 0.5 broadcast_in_dim.83
  95.8 99.7 %all_to_all.16 = bf16[8,128,2048]{2,1,0:T(8,128)(2,1)S(1)} all-to-all(bf16[8,128,2048]{2,1,0:T(8,128)(2,1)S(1)} %bitcast.103), channel_id=1, replica_groups=mesh['ctx'=8,'exp'=4] {'ctx'}, dimensions={0} | all-to-all | bytes 8388608 | tf_op jit(solution)/shard_map/all_to_all | solution.py:203
  195.6 2.0 copy-done.2
  197.6 2.5 fusion.30
  200.0 7.1 %convolution_convert_fusion = bf16[1024,2048]{1,0:T(8,128)(2,1)} fusion(bf16[1024,2048]{1,0:T(8,128)(2,1)} %bitcast.109, bf16[1,1,192,2048]{3,2,1,0:T(8,128)(2,1)S(1)} %copy-done, bf16[1,1,192,2048]{3,2,1,0:T(8,128)(2,1)S(1)} %copy-done.13, f32[1024,192]{0,1:T(8,128)} %fusion.30), kind=kOutput, calls=%fused_computation.43 | convolution fusion | flops 1613889536 | bytes 10747904 | tf_op jit(solution)/shard_map/dot_general | solution.py:210
  207.1 4.6 %all-to-all-start.2 = ((bf16[8,128,2048]{2,1,0:T(8,128)(2,1)}), bf16[8,128,2048]{2,1,0:T(8,128)(2,1)}, u32[]{:S(2)}, u32[]{:S(2)}) async-start(bf16[8,128,2048]{2,1,0:T(8,128)(2,1)} %bitcast.107), calls=%async_computation.2 | async-start | bytes 8388608 | tf_op jit(solution)/shard_map/all_to_all | solution.py:213
  211.7 92.2 %all-to-all-done.2 = bf16[8,128,2048]{2,1,0:T(8,128)(2,1)} async-done(((bf16[8,128,2048]{2,1,0:T(8,128)(2,1)}), bf16[8,128,2048]{2,1,0:T(8,128)(2,1)}, u32[]{:S(2)}, u32[]{:S(2)}) %all-to-all-start.2) | async-done | bytes 4194336 | tf_op jit(solution)/shard_map/all_to_all | solution.py:213
  304.0 3.1 reduce_sum.57
  307.0 0.8 dynamic-slice_bitcast_fusion
  307.8 0.6 collective-permute-start.1
  308.4 1.4 collective-permute-start.2
  309.8 6.6 %collective-permute-done = bf16[1,2,1,32,2048]{4,3,0,1,2:T(8,128)(2,1)} collective-permute-done((bf16[1,2,1,32,2048]{4,3,0,1,2:T(8,128)(2,1)}, bf16[1,2,1,32,2048]{4,3,0,1,2:T(8,128)(2,1)}, u32[]{:S(2)}, u32[]{:S(2)}) %collective-permute-start) | collective-permute-done | bytes 262176 | tf_op jit(solution)/shard_map/ppermute | solution.py:35
  316.4 1.0 constant_dynamic-update-slice_fusion.1
  317.4 1.0 constant_dynamic-update-slice_fusion
  318.4 2.0 collective-permute-done.2
  320.4 0.9 gather_fusion.1
  321.3 1.1 fusion.37
  (60 shorter events, 0.6 us)
Async XLA Ops:
  0.0 200.0 %copy-start = (bf16[1,1,192,2048]{3,2,1,0:T(8,128)(2,1)S(1)}, bf16[1,1,192,2048]{3,2,1,0:T(8,128)(2,1)}, u32[]{:S(2)}) copy-start(bf16[1,1,192,2048]{3,2,1,0:T(8,128)(2,1)} %param.23) | copy-start | bytes 2359300
  0.0 1.3 copy-start.8
  0.0 31.0 %copy-start.9 = (bf16[1,128,256]{2,1,0:T(8,128)(2,1)S(1)}, bf16[1,128,256]{2,1,0:T(8,128)(2,1)}, u32[]{:S(2)}) copy-start(bf16[1,128,256]{2,1,0:T(8,128)(2,1)} %param.18) | copy-start | bytes 196612
  61.1 3.4 %copy-start.3 = (f32[2,512,128]{2,1,0:T(8,128)S(1)}, f32[2,512,128]{2,1,0:T(8,128)}, u32[]{:S(2)}) copy-start(f32[2,512,128]{2,1,0:T(8,128)} %get-tuple-element.601) | copy-start | bytes 1572868 | tf_op jit(solution)/shard_map/while
  61.5 1.2 copy-start.5
  63.7 0.8 copy-start.6
  67.1 0.8 copy-start.4
  68.4 1.0 copy-start.3
  69.4 0.8 copy-start.4
  70.2 1.5 copy-start.7
  71.5 1.0 copy-start.1
  71.9 1.1 copy-start.10
  95.8 101.7 %copy-start.12 = (bf16[1,1,192,2048]{3,2,1,0:T(8,128)(2,1)S(1)}, bf16[1,1,192,2048]{3,2,1,0:T(8,128)(2,1)}, u32[]{:S(2)}) copy-start(bf16[1,1,192,2048]{3,2,1,0:T(8,128)(2,1)} %param.21) | copy-start | bytes 2359300
  195.6 2.0 copy-start.2
  197.6 2.5 copy-start.13
  207.1 96.9 %all-to-all-start.2 = ((bf16[8,128,2048]{2,1,0:T(8,128)(2,1)}), bf16[8,128,2048]{2,1,0:T(8,128)(2,1)}, u32[]{:S(2)}, u32[]{:S(2)}) async-start(bf16[8,128,2048]{2,1,0:T(8,128)(2,1)} %bitcast.107), calls=%async_computation.2 | async-start | bytes 8388608 | tf_op jit(solution)/shard_map/all_to_all | solution.py:213
  307.8 8.6 %collective-permute-start = (bf16[1,2,1,32,2048]{4,3,0,1,2:T(8,128)(2,1)}, bf16[1,2,1,32,2048]{4,3,0,1,2:T(8,128)(2,1)}, u32[]{:S(2)}, u32[]{:S(2)}) collective-permute-start(bf16[1,2,1,32,2048]{4,3,0,1,2:T(8,128)(2,1)} %get-tuple-element.455), channel_id=1, source_target_pairs={{0,1},{1,2},{2,3},{3,0},{4,5},{5,6},{6,7},{7,4},{8,9},{9,10},{10,1... | collective-permute-start | bytes 786440 | tf_op jit(solution)/shard_map/ppermute | solution.py:35
  307.8 9.6 %collective-permute-start.1 = (bf16[1,2,1,32,2048]{4,3,0,1,2:T(8,128)(2,1)S(1)}, bf16[1,2,1,32,2048]{4,3,0,1,2:T(8,128)(2,1)}, u32[]{:S(2)}, u32[]{:S(2)}) collective-permute-start(bf16[1,2,1,32,2048]{4,3,0,1,2:T(8,128)(2,1)S(1)} %get-tuple-element.454), channel_id=1, source_target_pairs={{0,2},{1,3},{2,0},{3,1},{4,6},{5,7},{6,4},{7,5},{8,10},{9,11},{10,... | collective-permute-start | bytes 786440 | tf_op jit(solution)/shard_map/ppermute | solution.py:35
  308.4 11.9 %collective-permute-start.2 = (bf16[1,2,1,32,2048]{4,3,0,1,2:T(8,128)(2,1)S(1)}, bf16[1,2,1,32,2048]{4,3,0,1,2:T(8,128)(2,1)S(1)}, u32[]{:S(2)}, u32[]{:S(2)}) collective-permute-start(bf16[1,2,1,32,2048]{4,3,0,1,2:T(8,128)(2,1)S(1)} %get-tuple-element.453), channel_id=1, source_target_pairs={{0,3},{1,0},{2,1},{3,2},{4,7},{5,4},{6,5},{7,6},{8,11},{9,8},{10,9... | collective-permute-start | bytes 786440 | tf_op jit(solution)/shard_map/ppermute | solution.py:35
  320.4 1.0 copy-start.11
